TPU v7x, 32 devices: a whole 2x2x4 slice. The times are simulated.
32 devices in a mesh: dp: 4 (over y, core), ctx: 8 (over z, x).
Axes of the slice: x: 2, y: 2, z: 4, core: 2. Of those that a mesh axis runs over, the one named last changes fastest.
Arguments:
- queries: bfloat16 [4608, 256], P(('dp', 'ctx')), parts along dimension 0, may hold values from -5 to 5
- keys: bfloat16 [4608, 256], P(('dp', 'ctx')), parts along dimension 0, may hold values from -5 to 5
- values: bfloat16 [4608, 256], P(('dp', 'ctx')), parts along dimension 0, may hold values from -2.5 to 2.5
- out_grad: bfloat16 [4608, 256], P(('dp', 'ctx')), parts along dimension 0, may hold values from -5 to 5
- span_end: int32 [4608], P(('dp', 'ctx')), parts along dimension 0, may hold values from 0 to 1152, as said below
Outputs:
- output: bfloat16 [4608, 256], P(('dp', 'ctx')), parts along dimension 0
- query_grad: float32 [4608, 256], P(('dp', 'ctx')), parts along dimension 0
- key_grad: float32 [4608, 256], P(('dp', 'ctx')), parts along dimension 0
- value_grad: float32 [4608, 256], P(('dp', 'ctx')), parts along dimension 0
There are 4 independent parts, one for each index of `dp`. A program takes and returns all parts, laid end to end along the dimension named above; each array names one. Nothing has to cross between parts.
Inputs may be any that keep to these rules, and one draw needn't show every extreme that they name: `span_end`: image spans are runs of consecutive tokens, each of at most 288 tokens; every token of a span holds the position just past the span's last token; the last 288 tokens of a document form one span.
All inputs are finite; a program needn't handle non-finite values.
Results may differ from a plain program's by a relative error of at most 0.035.
Values may be sent and summed in bfloat16 or wider, within the bound.
A program may use at most 64 MiB of HBM per device.

v0:
```python
import jax
import jax.numpy as jnp
from jax import lax
from jax.sharding import PartitionSpec as P

HEADS = 2
HEAD_DIM = 128


def split_heads(matrix):
    return matrix.reshape(matrix.shape[0], HEADS, HEAD_DIM)


def local(queries, keys, values, out_grad, span_end):
    row_count = queries.shape[0]
    scaling = HEAD_DIM ** (-0.5)
    device = lax.axis_index("ctx")
    base_positions = device * row_count + jnp.arange(row_count, dtype=jnp.int32)
    base_limits = jnp.maximum(base_positions + 1, span_end)
    limit_all = lax.all_gather(base_limits, "ctx", axis=0, tiled=True)
    query_rows_own, key_rows_own, value_rows_own, grad_rows_own = (queries, keys, values, out_grad)
    query_own = split_heads(query_rows_own)
    key_own = split_heads(key_rows_own)
    value_own = split_heads(value_rows_own)
    grad_own = split_heads(grad_rows_own)

    def own_scores(key_piece):
        columns = jnp.arange(key_piece.shape[0], dtype=jnp.int32)
        visible = (columns[None, :] < base_limits[:, None])[None]
        scores = (
            jnp.einsum("qhd,khd->hqk", query_own, key_piece, preferred_element_type=jnp.float32)
            * scaling
        )
        return (scores, visible)

    pieces = (
        lax.all_gather(keys, "ctx", axis=0, tiled=True),
        lax.all_gather(values, "ctx", axis=0, tiled=True),
    )
    run_high = jnp.full((HEADS, row_count), -1e30, jnp.float32)
    weighted = jnp.zeros((row_count, HEADS, HEAD_DIM), jnp.float32)
    key_piece = split_heads(pieces[0])
    value_piece = split_heads(pieces[1])
    scores, visible = own_scores(key_piece)
    scores = jnp.where(visible, scores, -1e30)
    new_high = jnp.maximum(run_high, jnp.max(scores, axis=-1))
    factor = jnp.exp(run_high - new_high)
    weights_now = jnp.where(visible, jnp.exp(scores - new_high[..., None]), 0.0)
    run_total = jnp.sum(weights_now, axis=-1)
    weighted = weighted * factor.T[:, :, None] + jnp.einsum(
        "hqk,khd->qhd",
        weights_now,
        value_piece.astype(jnp.float32),
        precision=lax.Precision.HIGHEST,
        preferred_element_type=jnp.float32,
    )
    run_high, run_total, weighted = (new_high, run_total, weighted)
    log_total = run_high + jnp.log(run_total)
    output = (weighted / run_total.T[:, :, None]).astype(jnp.bfloat16)
    row_dot = jnp.sum(grad_own.astype(jnp.float32) * output.astype(jnp.float32), axis=-1).T
    pieces = (
        lax.all_gather(keys, "ctx", axis=0, tiled=True),
        lax.all_gather(values, "ctx", axis=0, tiled=True),
    )
    key_piece = split_heads(pieces[0])
    value_piece = split_heads(pieces[1])
    scores, visible = own_scores(key_piece)
    probs = jnp.where(visible, jnp.exp(scores - log_total[..., None]), 0.0)
    prob_grad = jnp.einsum(
        "qhd,khd->hqk", grad_own, value_piece, preferred_element_type=jnp.float32
    )
    score_grad = probs * (prob_grad - row_dot[..., None])
    query_grad = jnp.einsum(
        "hqk,khd->qhd",
        score_grad.astype(jnp.bfloat16),
        key_piece,
        preferred_element_type=jnp.float32,
    )
    log_all, dot_all = (
        lax.all_gather(log_total, "ctx", axis=1, tiled=True),
        lax.all_gather(row_dot, "ctx", axis=1, tiled=True),
    )
    pieces = (
        lax.all_gather(queries, "ctx", axis=0, tiled=True),
        lax.all_gather(out_grad, "ctx", axis=0, tiled=True),
    )
    query_piece = split_heads(pieces[0])
    grad_piece = split_heads(pieces[1])
    visible = (base_positions[None, :] < limit_all[:, None])[None]
    scores = (
        jnp.einsum("qhd,khd->hqk", query_piece, key_own, preferred_element_type=jnp.float32)
        * scaling
    )
    probs = jnp.where(visible, jnp.exp(scores - log_all[..., None]), 0.0)
    value_grad = jnp.einsum(
        "hqk,qhd->khd", probs.astype(jnp.bfloat16), grad_piece, preferred_element_type=jnp.float32
    )
    prob_grad = jnp.einsum(
        "qhd,khd->hqk", grad_piece, value_own, preferred_element_type=jnp.float32
    )
    score_grad = probs * (prob_grad - dot_all[..., None])
    key_grad = jnp.einsum(
        "hqk,qhd->khd",
        score_grad.astype(jnp.bfloat16),
        query_piece,
        preferred_element_type=jnp.float32,
    )
    key_grad, value_grad = (key_grad, value_grad)
    flat_shape = (row_count, HEADS * HEAD_DIM)
    results = (
        output.astype(jnp.float32).reshape(flat_shape),
        (query_grad * scaling).reshape(flat_shape),
        (key_grad * scaling).reshape(flat_shape),
        value_grad.reshape(flat_shape),
    )
    return (results[0].astype(jnp.bfloat16), results[1], results[2], results[3])


def solution(mesh):
    in_specs = (
        P(("dp", "ctx"), None),
        P(("dp", "ctx"), None),
        P(("dp", "ctx"), None),
        P(("dp", "ctx"), None),
        P(("dp", "ctx")),
    )
    out_specs = (
        P(("dp", "ctx"), None),
        P(("dp", "ctx"), None),
        P(("dp", "ctx"), None),
        P(("dp", "ctx"), None),
    )
    return jax.shard_map(local, mesh=mesh, in_specs=in_specs, out_specs=out_specs, check_vma=False)
```

profile of v0, /device:TPU:0, one launch (start us, length us, event | category | flops | bytes accessed | tf_op | source)
XLA Modules:
  0.0 201.7 jit_solution(14404172331278344812)
XLA Ops:
  0.6 0.0 copy-start
  0.6 1.3 dynamic-slice
  2.6 0.8 fusion.42
  3.4 0.2 iota_compare_fusion
  3.6 33.4 %all_gather.23 = bf16[1152,256]{1,0:T(8,128)(2,1)S(1)} all-gather(bf16[144,256]{1,0:T(8,128)(2,1)} %param.6), channel_id=1, replica_groups=mesh['dp'=4,'ctx'=8] {'ctx'}, dimensions={0}, use_global_device_ids=true | all-gather | bytes 663552 | tf_op jit(solution)/shard_map/all_gather | solution.py:37
  37.0 0.3 copy.28
  37.3 0.0 copy-done
  37.3 0.0 copy-start.1
  37.3 0.5 select_reduce_fusion
  37.8 0.0 copy-start.2
  37.8 0.5 fusion.16
  38.3 31.5 %all_gather.24 = bf16[1152,256]{1,0:T(8,128)(2,1)S(1)} all-gather(bf16[144,256]{1,0:T(8,128)(2,1)S(1)} %copy-done.1), channel_id=1, replica_groups=mesh['dp'=4,'ctx'=8] {'ctx'}, dimensions={0}, use_global_device_ids=true | all-gather | bytes 663552 | tf_op jit(solution)/shard_map/all_gather | solution.py:38
  69.8 0.3 copy.31
  70.1 1.2 multiply_reduce_fusion
  71.4 0.6 copy_bitcast_fusion.3
  72.0 0.7 fusion.10
  72.8 0.7 copy.92
  73.4 31.7 %all_gather.28 = bf16[1152,256]{1,0:T(8,128)(2,1)S(1)} all-gather(bf16[144,256]{1,0:T(8,128)(2,1)S(1)} %copy-done.2), channel_id=1, replica_groups=mesh['dp'=4,'ctx'=8] {'ctx'}, dimensions={0}, use_global_device_ids=true | all-gather | bytes 663552 | tf_op jit(solution)/shard_map/all_gather | solution.py:85
  105.1 0.3 copy.43
  105.4 0.0 copy-start.3
  105.4 31.4 %all_gather.26 = bf16[1152,256]{1,0:T(8,128)(2,1)S(1)} all-gather(bf16[144,256]{1,0:T(8,128)(2,1)S(1)} %copy-done), channel_id=1, replica_groups=mesh['dp'=4,'ctx'=8] {'ctx'}, dimensions={0}, use_global_device_ids=true | all-gather | bytes 663552 | tf_op jit(solution)/shard_map/all_gather | solution.py:84
  136.8 0.3 copy.39
  137.1 26.1 %all-gather = f32[8,144,2]{1,2,0:T(2,128)S(1)} all-gather(f32[1,144,2]{1,2,0:T(2,128)S(1)} %bitcast.105), channel_id=1, replica_groups=mesh['dp'=4,'ctx'=8] {'ctx'}, dimensions={0}, use_global_device_ids=true | all-gather | bytes 10368 | tf_op jit(solution)/shard_map/all_gather | solution.py:80
  163.2 0.1 reshape.122
  163.3 9.9 %all-reduce = s32[1152]{0:T(1024)S(1)} all-reduce(s32[1152]{0:T(1024)S(1)} %get-tuple-element.4), channel_id=1, replica_groups=mesh['dp'=4,'ctx'=8] {'ctx'}, use_global_device_ids=true, to_apply=%add | all-reduce | flops 1152 | bytes 9216
  173.2 0.2 broadcast_compare_fusion
  173.4 0.5 fusion.4
  173.9 0.3 convolution_bitcast_fusion
  174.3 26.1 %all-gather.1 = f32[8,144,2]{1,2,0:T(2,128)S(1)} all-gather(f32[1,144,2]{1,2,0:T(2,128)S(1)} %bitcast.107), channel_id=1, replica_groups=mesh['dp'=4,'ctx'=8] {'ctx'}, dimensions={0}, use_global_device_ids=true | all-gather | bytes 10368 | tf_op jit(solution)/shard_map/all_gather | solution.py:81
  200.4 0.1 reshape.124
  200.5 0.5 fusion.12
  201.0 0.7 copy_bitcast_fusion
  (9 shorter events, 0.0 us)
Async XLA Ops:
  0.6 36.7 %copy-start = (bf16[144,256]{1,0:T(8,128)(2,1)S(1)}, bf16[144,256]{1,0:T(8,128)(2,1)}, u32[]{:S(2)}) copy-start(bf16[144,256]{1,0:T(8,128)(2,1)} %param.5) | copy-start | bytes 221188
  37.3 1.0 copy-start.1
  37.8 32.3 %copy-start.2 = (bf16[144,256]{1,0:T(8,128)(2,1)S(1)}, bf16[144,256]{1,0:T(8,128)(2,1)}, u32[]{:S(2)}) copy-start(bf16[144,256]{1,0:T(8,128)(2,1)} %param.8) | copy-start | bytes 221188
  105.4 68.0 %copy-start.3 = (bf16[144,256]{1,0:T(8,128)(2,1)S(1)}, bf16[144,256]{1,0:T(8,128)(2,1)}, u32[]{:S(2)}) copy-start(bf16[144,256]{1,0:T(8,128)(2,1)} %param.6) | copy-start | bytes 221188
where the time goes:
time: 202 us
  blocking collectives  190 us (94%)
  local copies, waits for them, and re-layouts  4.71 us (2%)
  matrix products  3.81 us (2%)
    all_gather x1, blocking collectives, local(): lax.all_gather(keys, 'ctx', axis=0, tiled=True)  33.4 us
    all_gather x1, blocking collectives, local(): lax.all_gather(out_grad, 'ctx', axis=0, tiled=True)  31.7 us
    all_gather x1, blocking collectives, local(): lax.all_gather(values, 'ctx', axis=0, tiled=True)  31.5 us
    all_gather x1, blocking collectives, local(): lax.all_gather(queries, 'ctx', axis=0, tiled=True)  31.4 us
    all_gather x1, blocking collectives, local(): lax.all_gather(log_total, 'ctx', axis=1, tiled=True)  26.1 us
    all_gather x1, blocking collectives, local(): lax.all_gather(row_dot, 'ctx', axis=1, tiled=True)  26.1 us
    unnamed x1, blocking collectives  9.9 us

commit v1 on v0

--- a/solution.py
+++ b/solution.py
@@ -5,6 +5,18 @@
 
 HEADS = 2
 HEAD_DIM = 128
+
+
+def gather_by_bits(x, axis, dim):
+    ways, here, turn = (lax.axis_size(axis), lax.axis_index(axis), x.shape[dim])
+    line, have = (x, 1)
+    while have < ways:
+        line = jnp.concatenate(
+            [line, lax.ppermute(line, axis, [(d, (d - have) % ways) for d in range(ways)])],
+            axis=dim,
+        )
+        have = 2 * have
+    return jnp.roll(line, here * turn, axis=dim)
 
 
 def split_heads(matrix):
@@ -77,7 +89,7 @@
         preferred_element_type=jnp.float32,
     )
     log_all, dot_all = (
-        lax.all_gather(log_total, "ctx", axis=1, tiled=True),
+        gather_by_bits(log_total, "ctx", 1),
         lax.all_gather(row_dot, "ctx", axis=1, tiled=True),
     )
     pieces = (

time: 202 us -> 185 us (0.916)
  blocking collectives: 190 us -> 163 us
  starting transfers between devices: 0 us -> 4.98 us
  matrix products: 3.81 us -> 6.45 us
    all_gather x1 -> x0, blocking collectives: 26.1 us -> none  [local(): lax.all_gather(log_total, 'ctx', axis=1, tiled=True)]
    ppermute x0 -> x3, starting transfers between devices: none -> 4.98 us  [gather_by_bits(): lax.ppermute(line, axis, [(d, (d - have) % ways) for d in range(ways)])]
  transfers between devices with their start and end apart: 0 -> 3, of which waited for: 0 -> 1; matrix products, arithmetic and copies ran while one was open for 0% -> 4% of each run, Pallas kernels for 0% -> 0%
where the time goes in v1:
time: 185 us
  blocking collectives  163 us (88%)
  matrix products  6.45 us (3%)
  local copies, waits for them, and re-layouts  5.61 us (3%)
  starting transfers between devices  4.98 us (3%)
    all_gather x1, blocking collectives, local(): lax.all_gather(keys, 'ctx', axis=0, tiled=True)  33.4 us
    all_gather x1, blocking collectives, local(): lax.all_gather(queries, 'ctx', axis=0, tiled=True)  31.6 us
    all_gather x1, blocking collectives, local(): lax.all_gather(values, 'ctx', axis=0, tiled=True)  31.5 us
    all_gather x1, blocking collectives, local(): lax.all_gather(out_grad, 'ctx', axis=0, tiled=True)  31.3 us
    all_gather x1, blocking collectives, local(): lax.all_gather(row_dot, 'ctx', axis=1, tiled=True)  26.2 us
    unnamed x1, blocking collectives  8.83 us
    ppermute x3, starting transfers between devices, gather_by_bits(): lax.ppermute(line, axis, [(d, (d - have) % ways) for d in range(ways)])  4.98 us
  transfers between devices with their start and end apart: 3, of which 1 were waited for; matrix products, arithmetic and copies ran while one was open for 4% of the time, Pallas kernels for 0%

profile of v1, /device:TPU:0, one launch (start us, length us, event | category | flops | bytes accessed | tf_op | source)
XLA Modules:
  0.0 185.0 jit_solution(11761370676163984736)
XLA Ops:
  0.6 1.3 dynamic-slice
  2.6 0.8 fusion.48
  3.4 0.2 iota_compare_fusion
  3.6 33.4 %all_gather.20 = bf16[1152,256]{1,0:T(8,128)(2,1)S(1)} all-gather(bf16[144,256]{1,0:T(8,128)(2,1)} %param.6), channel_id=1, replica_groups=mesh['dp'=4,'ctx'=8] {'ctx'}, dimensions={0}, use_global_device_ids=true | all-gather | bytes 663552 | tf_op jit(solution)/shard_map/all_gather | solution.py:49
  37.0 0.3 copy.28
  37.3 0.5 select_reduce_fusion
  37.8 0.5 fusion.14
  38.3 4.4 %collective-permute-start = (f32[2,144]{1,0:T(2,128)S(1)}, f32[2,144]{1,0:T(2,128)S(1)}, u32[]{:S(2)}, u32[]{:S(2)}) collective-permute-start(f32[2,144]{1,0:T(2,128)S(1)} %get-tuple-element.6), channel_id=1, source_target_pairs={{0,7},{1,0},{2,1},{3,2},{4,3},{5,4},{6,5},{7,6},{8,15},{9,8},{10,9... | collective-permute-start | bytes 3464 | tf_op jit(solution)/shard_map/ppermute | solution.py:15
  42.8 31.6 %all_gather.23 = bf16[1152,256]{1,0:T(8,128)(2,1)S(1)} all-gather(bf16[144,256]{1,0:T(8,128)(2,1)S(1)} %copy-done.1), channel_id=1, replica_groups=mesh['dp'=4,'ctx'=8] {'ctx'}, dimensions={0}, use_global_device_ids=true | all-gather | bytes 663552 | tf_op jit(solution)/shard_map/all_gather | solution.py:96
  74.4 31.5 %all_gather.21 = bf16[1152,256]{1,0:T(8,128)(2,1)S(1)} all-gather(bf16[144,256]{1,0:T(8,128)(2,1)S(1)} %copy-done.6), channel_id=1, replica_groups=mesh['dp'=4,'ctx'=8] {'ctx'}, dimensions={0}, use_global_device_ids=true | all-gather | bytes 663552 | tf_op jit(solution)/shard_map/all_gather | solution.py:50
  105.9 1.1 copy.31
  107.0 2.9 %multiply_reduce_fusion = (f32[144,2]{0,1:T(2,128)S(1)}, bf16[144,2,128]{2,0,1:T(8,128)(2,1)}) fusion(f32[144,2]{0,1:T(2,128)S(1)} %bitcast.97, bf16[1152,2,128]{0,2,1:T(8,128)(2,1)} %bitcast.93, f32[2,144,1152]{2,1,0:T(8,128)S(1)} %get-tuple-element.9, f32[2,144]{1,0:T(2,128)S(1)} %broadcast_maximum_fusion, pred[144,1152]{1,0:T(8,128)(4,1)S(1)} %iota_compare_fusion, ...), kind=kOutput, calls=%fused_computation.44 | convolution fusion | flops 510861024 | bytes 2234880 | tf_op jit(solution)/shard_map/hqk,khd->qhd/dot_general | solution.py:62
  109.8 1.7 fusion.7
  111.5 0.3 copy.39
  111.8 0.3 convolution_multiply_fusion
  112.2 8.8 %all-reduce = s32[1152]{0:T(1024)S(1)} all-reduce(s32[1152]{0:T(1024)S(1)} %get-tuple-element.4), channel_id=1, replica_groups=mesh['dp'=4,'ctx'=8] {'ctx'}, use_global_device_ids=true, to_apply=%add | all-reduce | flops 1152 | bytes 9216
  121.0 0.2 broadcast_compare_fusion
  121.2 31.3 %all_gather.24 = bf16[1152,256]{1,0:T(8,128)(2,1)S(1)} all-gather(bf16[144,256]{1,0:T(8,128)(2,1)S(1)} %copy-done.5), channel_id=1, replica_groups=mesh['dp'=4,'ctx'=8] {'ctx'}, dimensions={0}, use_global_device_ids=true | all-gather | bytes 663552 | tf_op jit(solution)/shard_map/all_gather | solution.py:97
  152.5 0.1 pad_maximum_fusion.1
  152.6 0.6 collective-permute-start.1
  153.2 0.6 copy_bitcast_fusion.3
  153.8 0.7 copy.91
  154.5 1.7 collective-permute-done.1
  156.2 0.1 pad_maximum_fusion
  156.3 0.3 copy.42
  156.6 26.2 %all-gather = f32[8,144,2]{1,2,0:T(2,128)S(1)} all-gather(f32[1,144,2]{1,2,0:T(2,128)S(1)} %bitcast.99), channel_id=1, replica_groups=mesh['dp'=4,'ctx'=8] {'ctx'}, dimensions={0}, use_global_device_ids=true | all-gather | bytes 10368 | tf_op jit(solution)/shard_map/all_gather | solution.py:93
  182.9 0.1 reshape.122
  183.0 0.1 concatenate.16
  183.1 0.1 constant_dynamic-slice_fusion
  183.2 0.4 convolution_bitcast_fusion
  183.6 0.7 fusion.9
  184.3 0.7 copy_bitcast_fusion
  (24 shorter events, 0.1 us)
Async XLA Ops:
  0.6 36.7 %copy-start.1 = (bf16[144,256]{1,0:T(8,128)(2,1)S(1)}, bf16[144,256]{1,0:T(8,128)(2,1)}, u32[]{:S(2)}) copy-start(bf16[144,256]{1,0:T(8,128)(2,1)} %param.5) | copy-start | bytes 221188
  37.8 36.6 %copy-start.6 = (bf16[144,256]{1,0:T(8,128)(2,1)S(1)}, bf16[144,256]{1,0:T(8,128)(2,1)}, u32[]{:S(2)}) copy-start(bf16[144,256]{1,0:T(8,128)(2,1)} %param.7) | copy-start | bytes 221188
  38.3 68.6 %copy-start.4 = (bf16[144,256]{1,0:T(8,128)(2,1)S(1)}, bf16[144,256]{1,0:T(8,128)(2,1)}, u32[]{:S(2)}) copy-start(bf16[144,256]{1,0:T(8,128)(2,1)} %param.8) | copy-start | bytes 221188
  38.3 114.2 %collective-permute-start = (f32[2,144]{1,0:T(2,128)S(1)}, f32[2,144]{1,0:T(2,128)S(1)}, u32[]{:S(2)}, u32[]{:S(2)}) collective-permute-start(f32[2,144]{1,0:T(2,128)S(1)} %get-tuple-element.6), channel_id=1, source_target_pairs={{0,7},{1,0},{2,1},{3,2},{4,3},{5,4},{6,5},{7,6},{8,15},{9,8},{10,9... | collective-permute-start | bytes 3464 | tf_op jit(solution)/shard_map/ppermute | solution.py:15
  106.9 2.9 %copy-start = (bf16[1152,256]{0,1:T(8,128)(2,1)S(1)}, bf16[1152,256]{0,1:T(8,128)(2,1)}, u32[]{:S(2)}) copy-start(bf16[1152,256]{0,1:T(8,128)(2,1)} %copy.31) | copy-start | bytes 1769476
  109.8 2.0 %copy-start.2 = (bf16[144,256]{1,0:T(8,128)(2,1)S(1)}, bf16[144,256]{1,0:T(8,128)(2,1)}, u32[]{:S(2)}) copy-start(bf16[144,256]{1,0:T(8,128)(2,1)} %param.6) | copy-start | bytes 221188
  111.8 9.4 %copy-start.5 = (bf16[144,256]{1,0:T(8,128)(2,1)S(1)}, bf16[144,256]{1,0:T(8,128)(2,1)}, u32[]{:S(2)}) copy-start(bf16[144,256]{1,0:T(8,128)(2,1)} %param.8) | copy-start | bytes 221188
  111.8 41.3 %copy-start.3 = (bf16[144,2,128]{2,0,1:T(8,128)(2,1)S(1)}, bf16[144,2,128]{2,0,1:T(8,128)(2,1)}, u32[]{:S(2)}) copy-start(bf16[144,2,128]{2,0,1:T(8,128)(2,1)} %get-tuple-element.11) | copy-start | bytes 221188
  152.6 3.6 %collective-permute-start.1 = (f32[2,288]{1,0:T(2,128)S(1)}, f32[2,288]{1,0:T(2,128)S(1)}, u32[]{:S(2)}, u32[]{:S(2)}) collective-permute-start(f32[2,288]{1,0:T(2,128)S(1)} %pad_maximum_fusion.1), channel_id=1, source_target_pairs={{0,6},{1,7},{2,0},{3,1},{4,2},{5,3},{6,4},{7,5},{8,14},{9,15},{10,... | collective-permute-start | bytes 6920 | tf_op jit(solution)/shard_map/ppermute | solution.py:15
  156.3 26.7 %collective-permute-start.2 = (f32[2,576]{1,0:T(2,128)S(1)}, f32[2,576]{1,0:T(2,128)S(1)}, u32[]{:S(2)}, u32[]{:S(2)}) collective-permute-start(f32[2,576]{1,0:T(2,128)S(1)} %pad_maximum_fusion), channel_id=1, source_target_pairs={{0,4},{1,5},{2,6},{3,7},{4,0},{5,1},{6,2},{7,3},{8,12},{9,13},{10,... | collective-permute-start | bytes 13832 | tf_op jit(solution)/shard_map/ppermute | solution.py:15
  156.6 27.0 %copy-start.7 = (bf16[144,256]{1,0:T(8,128)(2,1)S(1)}, bf16[144,256]{1,0:T(8,128)(2,1)}, u32[]{:S(2)}) copy-start(bf16[144,256]{1,0:T(8,128)(2,1)} %param.7) | copy-start | bytes 221188
